TPU v7x, 32 devices: a whole 2x2x4 slice. The times are simulated.
32 devices in a mesh: dp: 16 (over z, y, x), sub: 2 (over core).
Axes of the slice: x: 2, y: 2, z: 4, core: 2. Of those that a mesh axis runs over, the one named last changes fastest.
Arguments:
- points: bfloat16 [16384, 256], P(('dp', 'sub'))
- candidates: int32 [4, 768], replicated, may hold values from 0 to 16383, as said below
- owner_slot: int32 [3072], replicated, may hold values from 0 to 3071, each once
Outputs:
- centroids: float32 [3072, 256], P(('dp', 'sub'))
- masses: float32 [3072], P(('dp', 'sub'))
- min_dist: float32 [16384], P(('dp', 'sub'))
Inputs may be any that keep to these rules, and one draw needn't show every extreme that they name: In each round the candidates are distinct rows; no device's block of 512 rows holds more than 96 candidates of one round, and in each round some device's block holds exactly 96.
All inputs are finite; a program needn't handle non-finite values.
Results may differ from a plain program's by a relative error of at most 0.00055.
Values may be sent and summed in bfloat16 or wider, within the bound.
No kernel may reach another device: no remote copies, remote signals or barrier semaphores. Data moves between devices by JAX's collectives and lax.ppermute only.
A program may use at most 64 MiB of HBM per device.

v0:
```python
import jax
import jax.numpy as jnp
from jax import lax
from jax.sharding import PartitionSpec as P


def pick_rows(round_rows, points, my_device):
    row_count = points.shape[0]
    flat_rows = round_rows.reshape(-1)
    owner_dev = flat_rows // row_count
    local_row = flat_rows % row_count
    mine = owner_dev == my_device
    picked = jnp.where(
        mine[:, None], points[local_row].astype(jnp.float32), jnp.zeros((), jnp.float32)
    )
    return lax.psum(picked, ("dp", "sub")).astype(jnp.bfloat16)


def on_device(points, candidates, owner_slot):
    row_count = points.shape[0]
    width_dim = points.shape[1]
    round_count = candidates.shape[0]
    cand_count = candidates.shape[1]
    my_device = lax.axis_index(("dp", "sub"))
    block_rows = min(512, row_count)
    point_norm = jnp.sum(points.astype(jnp.float32) ** 2, axis=1)
    all_chosen = pick_rows(candidates, points, my_device)
    chosen_list = [
        all_chosen[which_round * cand_count : (which_round + 1) * cand_count]
        for which_round in range(round_count)
    ]
    nearest_parts = [jnp.full((block_rows,), 3e38, jnp.float32)]
    sums_parts = []
    mass_parts = []
    for which_round in range(round_count):
        chosen = chosen_list[which_round]
        cand_norm = jnp.sum(chosen.astype(jnp.float32) ** 2, axis=1)
        dots = lax.dot_general(
            points, chosen, (((1,), (1,)), ((), ())), preferred_element_type=jnp.float32
        )
        dist = point_norm[:, None] + cand_norm[None, :] - 2.0 * dots
        nearest_parts[0] = jnp.minimum(nearest_parts[0], jnp.min(dist, axis=1))
        kernel = jnp.exp(-dist / 0.25).astype(jnp.bfloat16)
        sums_round = lax.dot_general(
            kernel, points, (((0,), (0,)), ((), ())), preferred_element_type=jnp.float32
        )
        mass_round = jnp.sum(kernel.astype(jnp.float32), axis=0)
        sums_parts.append(sums_round)
        mass_parts.append(mass_round)
    partial_sums = jnp.concatenate(sums_parts, axis=0)
    partial_mass = jnp.concatenate(mass_parts, axis=0)
    total_rows = partial_sums.shape[0]
    placed_sums = jnp.zeros((total_rows, width_dim), jnp.float32).at[owner_slot].set(partial_sums)
    placed_mass = jnp.zeros((total_rows,), jnp.float32).at[owner_slot].set(partial_mass)
    summed, masses = (
        lax.psum_scatter(placed_sums, ("dp", "sub"), scatter_dimension=0, tiled=True),
        lax.psum_scatter(placed_mass, ("dp", "sub"), scatter_dimension=0, tiled=True),
    )
    centroids = summed / masses[:, None]
    min_dist = nearest_parts[0]
    return (centroids, masses, min_dist)


def solution(mesh):
    placed = (P(("dp", "sub"), None), P(), P())
    return jax.shard_map(
        on_device,
        mesh=mesh,
        in_specs=placed,
        out_specs=(P(("dp", "sub"), None), P(("dp", "sub")), P(("dp", "sub"))),
        check_vma=False,
    )
```

profile of v0, /device:TPU:0, one launch (start us, length us, event | category | flops | bytes accessed | tf_op | source)
XLA Modules:
  0.0 239.9 jit_solution(6603793152134570887)
XLA Ops:
  7.2 0.0 copy-start
  7.2 0.0 reduce-scatter.2.cloned.1.call-start
  7.2 0.7 compare_select_fusion.3
  8.0 0.7 reshape.107
  8.7 0.7 copy.6
  9.4 0.1 compare_select_fusion
  9.5 1.1 multiply_reduce_fusion.4
  10.6 0.0 copy-done
  10.6 13.0 %gather_fusion = bf16[3072,256]{1,0:T(8,128)(2,1)} fusion(bf16[512,256]{1,0:T(8,128)(2,1)S(1)} %copy-done, s32[3072]{0:T(1024)S(1)} %broadcast_clamp_fusion), kind=kCustom, calls=%fused_computation | custom fusion | bytes 3158016 | tf_op jit(solution)/shard_map/gather | solution.py:14
  23.6 2.7 %convert_select_fusion = f32[3072,256]{1,0:T(8,128)S(1)} fusion(bf16[3072,256]{1,0:T(8,128)(2,1)} %gather_fusion, pred[3072]{0:T(1024)(128)(4,1)S(1)} %fusion.18), kind=kLoop, calls=%fused_computation.11 | loop fusion | flops 1572864 | bytes 4721664 | tf_op jit(solution)/shard_map/jit(_where)/select_n | solution.py:13
  26.3 80.7 %all-reduce.2 = bf16[3072,256]{1,0:T(8,128)(2,1)} all-reduce(f32[3072,256]{1,0:T(8,128)S(1)} %convert_select_fusion), channel_id=1, replica_groups=mesh['dp'=16,'sub'=2] {'dp','sub'}, use_global_device_ids=true, to_apply=%region_1.2 | all-reduce | flops 786432 | bytes 4718592 | tf_op jit(solution)/shard_map/psum | solution.py:16
  107.0 0.0 copy-start.1
  107.0 1.9 multiply_reduce_fusion.3
  108.9 0.0 copy-done.1
  109.0 0.7 fusion.30
  109.6 0.4 fusion.16
  110.0 0.7 fusion.29
  110.7 0.4 fusion.15
  111.1 0.7 fusion.28
  111.8 0.4 fusion.14
  112.2 0.7 fusion.27
  112.9 0.4 fusion.13
  113.3 17.1 %scatter_custom_fusion = f32[3072,256]{1,0:T(8,128)} fusion(s32[3072]{0:T(1024)S(1)} %compare_select_fusion.3, f32[768,256]{1,0:T(8,128)S(1)} %fusion.16, f32[]{:T(128)} %constant.61, f32[768,256]{1,0:T(8,128)S(1)} %fusion.15, f32[768,256]{1,0:T(8,128)S(1)} %fusion.14, f32[768,256]{1,0:T(8,128)S(1)} %fusion.13, f32[]{:T(128)} %constant.43.clone.1), kind=kCustom, calls=%fused_computation.3 | custom fusion | flops 2359296 | bytes 6291464 | tf_op jit(solution)/shard_map/scatter | solution.py:53
  130.4 0.0 reduce-scatter.2.cloned.1.call-update
  130.4 11.8 %scatter_custom_fusion.1 = f32[3072]{0:T(1024)S(1)} fusion(s32[3072]{0:T(1024)S(1)} %compare_select_fusion.3, f32[3072]{0:T(1024)S(1)} %pad_maximum_fusion, f32[]{:T(128)} %constant.43.clone.1), kind=kCustom, calls=%fused_computation.55 | custom fusion | bytes 12292 | tf_op jit(solution)/shard_map/scatter | solution.py:54
  142.3 38.4 %all-reduce = f32[3072]{0:T(1024)S(1)} all-reduce(f32[3072]{0:T(1024)S(1)} %scatter_custom_fusion.1), channel_id=3, replica_groups=mesh['dp'=16,'sub'=2] {'dp','sub'}, use_global_device_ids=true, to_apply=%region_13.14.clone | all-reduce | flops 3072 | bytes 24576
  180.6 0.1 dynamic-slice
  180.7 0.0 copy-start.2
  180.7 0.6 minimum_minimum_fusion
  181.3 50.1 %reduce-scatter.2.cloned.1.call-done = f32[96,256]{1,0:T(8,128)} async-done(((f32[3072,256]{1,0:T(8,128)}), f32[96,256]{1,0:T(8,128)}) %reduce-scatter.2.cloned.1.call-update) | async-done | bytes 98320 | tf_op jit(solution)/shard_map/reduce_scatter | solution.py:56
  231.4 1.6 broadcast_divide_fusion
  233.0 0.0 copy-done.2
  (3 shorter events, 0.0 us)
Async XLA Ops:
  7.2 3.4 %copy-start = (bf16[512,256]{1,0:T(8,128)(2,1)S(1)}, bf16[512,256]{1,0:T(8,128)(2,1)}, u32[]{:S(2)}) copy-start(bf16[512,256]{1,0:T(8,128)(2,1)} %param.3) | copy-start | bytes 786436
  7.2 224.2 %reduce-scatter.2.cloned.1.call-start = ((), (), s32[]{:S(2)}) async-start(), calls=%async_computation.1 | async-start | bytes 3244032 | tf_op jit(solution)/shard_map/reduce_scatter | solution.py:56
  107.0 2.0 copy-start.1
  180.7 52.3 %copy-start.2 = (f32[96]{0:T(128)}, f32[96]{0:T(128)S(1)}, u32[]{:S(2)}) copy-start(f32[96]{0:T(128)S(1)} %dynamic-slice) | copy-start | bytes 1156
Sparse Core Ops, SparseCore 0:
  130.5 100.8 reduce-scatter.1
where the time goes:
time: 240 us
  blocking collectives  119 us (50%)
  waiting for transfers between devices  50.1 us (21%)
  local copies, waits for them, and re-layouts  26.3 us (11%)
  other arithmetic  25.9 us (11%)
  between operations  14.2 us (6%)
  matrix products  4.27 us (2%)
    psum x1, blocking collectives, pick_rows(): return lax.psum(picked, ('dp', 'sub')).astype(jnp.bfloat16)  80.7 us
    reduce_scatter x1, waiting for transfers between devices, on_device(): lax.psum_scatter(placed_sums, ('dp', 'sub'), scatter_dimension=0, tiled=T...  50.1 us
    unnamed x1, blocking collectives  38.4 us
    scatter x1, other arithmetic, on_device(): jnp.zeros((total_rows, width_dim), jnp.float32).at[owner_slot]  17.1 us
    gather x1, local copies, waits for them, and re-layouts, pick_rows(): points[local_row].astype(jnp.float32)  13 us
    scatter x1, local copies, waits for them, and re-layouts, on_device(): jnp.zeros((total_rows,), jnp.float32).at[owner_slot].set(partial_mass)  11.8 us
  transfers between devices with their start and end apart: 1, of which 1 were waited for; matrix products, arithmetic and copies ran while one was open for 5% of the time, Pallas kernels for 0%

commit v1 on v0

--- a/solution.py
+++ b/solution.py
@@ -13,7 +13,13 @@
     picked = jnp.where(
         mine[:, None], points[local_row].astype(jnp.float32), jnp.zeros((), jnp.float32)
     )
-    return lax.psum(picked, ("dp", "sub")).astype(jnp.bfloat16)
+
+    def fix_heaps_by_axis(target):
+        for t in ("sub", "dp"):
+            target = lax.psum(target, axis_name=t)
+        return target
+
+    return fix_heaps_by_axis(picked).astype(jnp.bfloat16)
 
 
 def on_device(points, candidates, owner_slot):

time: 240 us -> 323 us (1.35)
  blocking collectives: 119 us -> 181 us
  waiting for transfers between devices: 50.1 us -> 73.9 us
    psum x1, blocking collectives: 80.7 us -> 140 us  [fix_heaps_by_axis(): target = lax.psum(target, axis_name=t)]
    psum x0 -> x1, waiting for transfers between devices: none -> 25.1 us  [fix_heaps_by_axis(): target = lax.psum(target, axis_name=t)]
  transfers between devices with their start and end apart: 1 -> 2, of which waited for: 1 -> 2; matrix products, arithmetic and copies ran while one was open for 5% -> 4% of each run, Pallas kernels for 0% -> 0%
where the time goes in v1:
time: 323 us; the launch traced here: 322 us
  blocking collectives  181 us (56%)
  waiting for transfers between devices  73.9 us (23%)
  local copies, waits for them, and re-layouts  25.7 us (8%)
  other arithmetic  22.8 us (7%)
  between operations  14.2 us (4%)
  matrix products  5.12 us (2%)
    psum x1, blocking collectives, fix_heaps_by_axis(): target = lax.psum(target, axis_name=t)  140 us
    reduce_scatter x1, waiting for transfers between devices, on_device(): lax.psum_scatter(placed_sums, ('dp', 'sub'), scatter_dimension=0, tiled=T...  48.8 us
    unnamed x1, blocking collectives  40.8 us
    psum x1, waiting for transfers between devices, fix_heaps_by_axis(): target = lax.psum(target, axis_name=t)  25.1 us
    scatter x1, other arithmetic, on_device(): jnp.zeros((total_rows, width_dim), jnp.float32).at[owner_slot]  17.1 us
    scatter x1, local copies, waits for them, and re-layouts, on_device(): jnp.zeros((total_rows,), jnp.float32).at[owner_slot].set(partial_mass)  11.8 us
    gather x1, local copies, waits for them, and re-layouts, pick_rows(): points[local_row].astype(jnp.float32)  10.8 us
  transfers between devices with their start and end apart: 2, of which 2 were waited for; matrix products, arithmetic and copies ran while one was open for 4% of the time, Pallas kernels for 0%

profile of v1, /device:TPU:0, one launch (start us, length us, event | category | flops | bytes accessed | tf_op | source)
XLA Modules:
  0.0 322.5 jit_solution(817018153103667169)
XLA Ops:
  7.2 0.0 all-reduce.4.cloned.1.call-start
  7.2 0.7 reshape.107
  7.9 0.7 copy.6
  8.7 0.1 compare_select_fusion
  8.7 10.8 %gather_fusion = bf16[3072,256]{1,0:T(8,128)(2,1)S(1)} fusion(bf16[512,256]{1,0:T(8,128)(2,1)} %param.3, s32[3072]{0:T(1024)S(1)} %broadcast_clamp_fusion), kind=kCustom, calls=%fused_computation | custom fusion | bytes 3158016 | tf_op jit(solution)/shard_map/gather | solution.py:14
  19.6 2.8 convert_select_fusion
  22.3 0.0 all-reduce.4.cloned.1.call-update
  22.4 0.0 reduce-scatter.2.cloned.1.call-start
  22.4 0.9 copy-done
  23.3 0.1 multiply_reduce_fusion.4
  23.4 0.0 copy-done.2
  23.5 25.1 %all-reduce.4.cloned.1.call-done = f32[3072,256]{1,0:T(8,128)} async-done(((f32[3072,256]{1,0:T(8,128)}), f32[3072,256]{1,0:T(8,128)}) %all-reduce.4.cloned.1.call-update) | async-done | bytes 3145744 | tf_op jit(solution)/shard_map/psum | solution.py:19
  48.5 139.8 %all-reduce.5 = bf16[3072,256]{1,0:T(8,128)(2,1)S(1)} all-reduce(f32[3072,256]{1,0:T(8,128)} %all-reduce.4.cloned.1.call-done), channel_id=1, replica_groups=mesh['dp'=16,'sub'=2] {'dp'}, use_global_device_ids=true, to_apply=%region_2.3 | all-reduce | flops 786432 | bytes 4718592 | tf_op jit(solution)/shard_map/psum | solution.py:19
  188.4 0.5 multiply_reduce_fusion.3
  188.9 0.7 fusion.30
  189.6 0.4 fusion.16
  189.9 0.7 fusion.29
  190.6 0.4 fusion.15
  191.0 0.7 fusion.28
  191.7 1.3 fusion.14
  193.0 0.7 fusion.27
  193.6 0.0 copy-start.1
  193.7 0.4 fusion.13
  194.0 0.7 copy-done.1
  194.8 17.1 %scatter_custom_fusion = f32[3072,256]{1,0:T(8,128)} fusion(s32[3072]{0:T(1024)S(1)} %compare_select_fusion.3, f32[768,256]{1,0:T(8,128)S(1)} %fusion.16, f32[]{:T(128)} %constant.61, f32[768,256]{1,0:T(8,128)S(1)} %fusion.15, f32[768,256]{1,0:T(8,128)S(1)} %copy-done.1, f32[768,256]{1,0:T(8,128)S(1)} %fusion.13, f32[]{:T(128)} %constant.43.clone.1), kind=kCustom, calls=%fused_computation.3 | custom fusion | flops 2359296 | bytes 6291464 | tf_op jit(solution)/shard_map/scatter | solution.py:59
  211.9 0.0 reduce-scatter.2.cloned.1.call-update
  212.0 11.8 %scatter_custom_fusion.1 = f32[3072]{0:T(1024)S(1)} fusion(s32[3072]{0:T(1024)S(1)} %compare_select_fusion.3, f32[3072]{0:T(1024)S(1)} %pad_maximum_fusion, f32[]{:T(128)} %constant.43.clone.1), kind=kCustom, calls=%fused_computation.55 | custom fusion | bytes 12292 | tf_op jit(solution)/shard_map/scatter | solution.py:60
  223.8 40.8 %all-reduce = f32[3072]{0:T(1024)S(1)} all-reduce(f32[3072]{0:T(1024)S(1)} %scatter_custom_fusion.1), channel_id=3, replica_groups=mesh['dp'=16,'sub'=2] {'dp','sub'}, use_global_device_ids=true, to_apply=%region_14.15.clone | all-reduce | flops 3072 | bytes 24576
  264.6 0.1 dynamic-slice
  264.6 0.6 minimum_minimum_fusion
  265.2 48.8 %reduce-scatter.2.cloned.1.call-done = f32[96,256]{1,0:T(8,128)} async-done(((f32[3072,256]{1,0:T(8,128)}), f32[96,256]{1,0:T(8,128)}) %reduce-scatter.2.cloned.1.call-update) | async-done | bytes 98320 | tf_op jit(solution)/shard_map/reduce_scatter | solution.py:62
  314.0 1.6 broadcast_divide_fusion
  (8 shorter events, 0.0 us)
Async XLA Ops:
  7.2 41.4 %all-reduce.4.cloned.1.call-start = ((), (), s32[]{:S(2)}) async-start(), calls=%async_computation.1 | async-start | bytes 6291456 | tf_op jit(solution)/shard_map/psum | solution.py:19
  22.3 0.9 copy-start
  22.3 1.1 copy-start.2
  22.4 291.7 %reduce-scatter.2.cloned.1.call-start = ((), (), s32[]{:S(2)}) async-start(), calls=%async_computation.2 | async-start | bytes 3244032 | tf_op jit(solution)/shard_map/reduce_scatter | solution.py:62
  193.6 1.1 copy-start.1
  264.6 51.0 %copy-start.3 = (f32[96]{0:T(128)}, f32[96]{0:T(128)S(1)}, u32[]{:S(2)}) copy-start(f32[96]{0:T(128)S(1)} %dynamic-slice) | copy-start | bytes 1156
Sparse Core Ops, SparseCore 0:
  22.5 26.0 all-reduce.3
  212.1 101.9 reduce-scatter.1
